TPU v7x, 512 devices: a whole 4x4x16 slice. The times are simulated.
512 devices in a mesh: ctx: 64 (over y, z_lo, core), exp: 8 (over z_hi, x).
Axes of the slice: x: 4, y: 4, z: 16 (z_hi: 2, z_lo: 8; z = z_hi * 8 + z_lo), core: 2. Of those that a mesh axis runs over, the one named last changes fastest.
Arguments:
- queries: bfloat16 [8192, 32, 128], P('ctx', 'exp'), may hold values from -100 to 100
- keys: bfloat16 [8192, 2, 128], P('ctx'), may hold values from -4 to 4
- values: bfloat16 [8192, 2, 128], P('ctx'), may hold values from -4 to 4
- resid: bfloat16 [8192, 4096], P('ctx', 'exp'), may hold values from -20 to 20
- gain: float32 [4096], P('exp'), may hold values from 0.1 to 1.9
- expert_ids: int32 [8192, 8], P('ctx'), may hold values from 0 to 127, all different within a row; in each aligned block of 128 rows (0 to 127, 128 to 255, ...) at most 10 rows name the same one
- gate_scores: float32 [8192, 8], P('ctx'), may hold values from 0.05 to 1
- w_gate_up: bfloat16 [64, 4096, 2, 768], P('ctx', 'exp'), may hold values from -0.09375 to 0.09375
- w_down: bfloat16 [64, 768, 4096], P('ctx', None, 'exp'), may hold values from -0.625 to 0.625
- w_out: bfloat16 [32, 128, 4096], P('exp', 'ctx'), may hold values from -0.5 to 0.5
Outputs:
- context: bfloat16 [8192, 32, 128], P('ctx', 'exp')
- mixed: bfloat16 [8192, 4096], P('ctx', 'exp')
Inputs may be any that keep to these rules, and one draw needn't show every extreme that they name: `expert_ids`: each row names 8 different experts; within the 128 rows of one index of ctx no expert is named more than 10 times.
All inputs are finite; a program needn't handle non-finite values.
Results may differ from a plain program's by a relative error of at most 0.02.
Values may be sent and summed in bfloat16 or wider, within the bound.
No kernel may reach another device: no remote copies, remote signals or barrier semaphores. Data moves between devices by JAX's collectives and lax.ppermute only.
A program may use at most 64 MiB of HBM per device.

v0:
```python
import math
import jax
import jax.numpy as jnp
from jax import lax
from jax.sharding import PartitionSpec as P

D = 4096
HQ = 32
KVH = 2
EXPERTS = 128
TOPK = 8
masked_score = -1e30
epsilon = 1e-06


def attend_piece(state_now, pair_piece, offset, query_rows, query_pos, last_pos, scaling):
    key_piece, value_piece = pair_piece
    length = key_piece.shape[0]

    def compute(state_in):
        running, denominator, numerator = state_in
        scores = (
            jnp.einsum("rd,kd->rk", query_rows, key_piece, preferred_element_type=jnp.float32)
            * scaling
        )
        key_pos = jnp.arange(length, dtype=jnp.int32)
        visible = key_pos[None, :] <= query_pos[:, None]
        masked = jnp.where(visible, scores, masked_score)
        highest = jnp.maximum(running, jnp.max(masked, axis=1))
        weights_exp = jnp.where(visible, jnp.exp(masked - highest[:, None]), 0.0)
        rounded = weights_exp.astype(jnp.bfloat16)
        numerator = jnp.dot(rounded, value_piece, preferred_element_type=jnp.float32)
        denominator = jnp.sum(weights_exp, axis=1)
        return (highest, denominator, numerator)

    def untouched(state_in):
        return state_in

    return lax.cond(offset <= last_pos, compute, untouched, state_now)


def body(queries, keys, values, resid, gain, expert_ids, gate_scores, w_gate_up, w_down, w_out):
    tokens_here = queries.shape[0]
    heads_here = queries.shape[1]
    head_size = queries.shape[2]
    ctx_count = lax.axis_size("ctx")
    ctx_place = lax.axis_index("ctx")
    exp_place = lax.axis_index("exp")
    own_pos = ctx_place * tokens_here + jnp.arange(tokens_here, dtype=jnp.int32)
    query_sets = (queries, own_pos)
    group_index = exp_place * heads_here // (HQ // KVH)
    key_local = lax.dynamic_index_in_dim(keys, group_index, 1, keepdims=False)
    value_local = lax.dynamic_index_in_dim(values, group_index, 1, keepdims=False)
    scaling = 1.0 / math.sqrt(head_size)
    set_queries, set_pos = query_sets
    set_rows = set_queries.shape[0] * heads_here
    initial = [
        (
            jnp.full((set_rows,), masked_score, jnp.float32),
            jnp.zeros((set_rows,), jnp.float32),
            jnp.zeros((set_rows, head_size), jnp.float32),
        )
    ]
    rows_set = set_queries.reshape(set_rows, head_size)
    pos_set = jnp.repeat(set_pos, heads_here)
    last_set = jnp.max(set_pos)
    updated = [
        attend_piece(
            tuple(initial)[0],
            (
                lax.all_gather(key_local, "ctx", axis=0, tiled=True),
                lax.all_gather(value_local, "ctx", axis=0, tiled=True),
            ),
            jnp.int32(0),
            rows_set,
            pos_set,
            last_set,
            scaling,
        )
    ]
    folded = tuple(updated)
    pieces_out = []
    for state_set in folded:
        normalized = state_set[2] / state_set[1][:, None]
        pieces_out.append(normalized.reshape(-1, heads_here, head_size).astype(jnp.bfloat16))
    context = pieces_out[0]
    whole_out = lax.all_gather(w_out, "ctx", axis=1, tiled=True)
    projected = jnp.einsum("thp,hpd->td", context, whole_out, preferred_element_type=jnp.float32)
    attended = lax.psum_scatter(
        projected.astype(jnp.bfloat16), "exp", scatter_dimension=1, tiled=True
    ).astype(jnp.float32)
    hidden_state = resid.astype(jnp.float32) + attended
    square_sum = lax.psum(jnp.sum(hidden_state * hidden_state, axis=1), "exp")
    inverse = lax.rsqrt(square_sum / D + epsilon)
    normed = (hidden_state * inverse[:, None] * gain[None, :]).astype(jnp.bfloat16)
    capacity = max(2, 5 * tokens_here * TOPK // (4 * EXPERTS))
    flat_ids = expert_ids.reshape(-1)
    onehot = (flat_ids[:, None] == jnp.arange(ctx_count, dtype=jnp.int32)[None, :]).astype(
        jnp.int32
    )
    earlier = jnp.cumsum(onehot, axis=0) - onehot
    rank_of = jnp.sum(earlier * onehot, axis=1)
    active = flat_ids < ctx_count
    slot_of = jnp.where(active, flat_ids * capacity + rank_of, -1).reshape(tokens_here, TOPK)
    slot_range = jnp.arange(ctx_count * capacity, dtype=jnp.int32)
    dispatch_map = jnp.zeros((ctx_count * capacity, tokens_here), jnp.bfloat16)
    for column in range(TOPK):
        dispatch_map = dispatch_map + (slot_range[:, None] == slot_of[None, :, column]).astype(
            jnp.bfloat16
        )
    local_width = normed.shape[1]
    outgoing = jnp.dot(dispatch_map, normed, preferred_element_type=jnp.float32).astype(
        jnp.bfloat16
    )
    outgoing = outgoing.reshape(ctx_count, capacity, local_width)
    arrived = lax.all_to_all(outgoing, "ctx", split_axis=0, concat_axis=0, tiled=True)
    sources = arrived.shape[0]
    width_slots = arrived.shape[1]
    row_block = arrived.reshape(sources * width_slots, local_width)
    partial_sum = jnp.einsum(
        "rd,dgf->rgf", row_block, w_gate_up[0], preferred_element_type=jnp.float32
    )
    summed = lax.psum(partial_sum.astype(jnp.bfloat16), "exp").astype(jnp.float32)
    hidden_units = (jax.nn.silu(summed[:, 0]) * summed[:, 1]).astype(jnp.bfloat16)
    result = jnp.dot(hidden_units, w_down[0], preferred_element_type=jnp.float32).astype(
        jnp.bfloat16
    )
    result = result.reshape(sources, width_slots, local_width)
    returned = lax.all_to_all(result, "ctx", split_axis=0, concat_axis=0, tiled=True)
    back_rows = returned.reshape(ctx_count * capacity, local_width)
    picked = jnp.take(back_rows, jnp.maximum(slot_of, 0).reshape(-1), axis=0).reshape(
        tokens_here, TOPK, local_width
    )
    weight_now = gate_scores / jnp.sum(gate_scores, axis=1, keepdims=True)
    weight_now = jnp.where(active.reshape(tokens_here, TOPK), weight_now, 0.0)
    routed = jnp.zeros((tokens_here, local_width), jnp.float32)
    for column in range(TOPK):
        routed = routed + weight_now[:, column : column + 1] * picked[:, column].astype(jnp.float32)
    mixed = (hidden_state + routed).astype(jnp.bfloat16)
    return (context, mixed)


def solution(mesh):
    in_specs = (
        P("ctx", "exp", None),
        P("ctx", None, None),
        P("ctx", None, None),
        P("ctx", "exp"),
        P("exp"),
        P("ctx", None),
        P("ctx", None),
        P("ctx", "exp", None, None),
        P("ctx", None, "exp"),
        P("exp", "ctx", None),
    )
    out_specs = (P("ctx", "exp", None), P("ctx", "exp"))
    return jax.shard_map(body, mesh=mesh, in_specs=in_specs, out_specs=out_specs, check_vma=False)
```

profile of v0, /device:TPU:7, one launch (start us, length us, event | category | flops | bytes accessed | tf_op | source)
XLA Modules:
  0.0 899.9 jit_solution(3959203209659631209)
XLA Ops:
  10.6 1.5 copy.72
  13.4 122.9 %all-gather.8.cloned.1.call-done = bf16[8192,1,128]{2,0,1:T(8,128)(2,1)} async-done(((bf16[128,1,128]{2,0,1:T(8,128)(2,1)}), bf16[8192,1,128]{2,0,1:T(8,128)(2,1)}) %all-gather.8.cloned.1.call-update) | async-done | bytes 2097168 | tf_op jit(solution)/shard_map/all_gather | solution.py:71
  136.3 118.7 %all-gather.10.cloned.1.call-done = bf16[8192,1,128]{2,0,1:T(8,128)(2,1)} async-done(((bf16[128,1,128]{2,0,1:T(8,128)(2,1)}), bf16[8192,1,128]{2,0,1:T(8,128)(2,1)}) %all-gather.10.cloned.1.call-update) | async-done | bytes 2097168 | tf_op jit(solution)/shard_map/all_gather | solution.py:72
  255.0 16.5 %conditional.1 = (f32[512]{0:T(512)S(1)}, f32[512,128]{1,0:T(8,128)S(1)}) conditional(s32[]{:T(128)} %convert_element_type.124, () %tuple.16, (s32[128]{0:T(128)S(1)}, bf16[128,4,128]{2,1,0:T(4,128)(2,1)}, bf16[8192,128]{1,0:T(8,128)(2,1)}, bf16[8192,128]{1,0:T(8,128)(2,1)}) %tuple.48), branch_computations={%region_1.2_spmd, %region_2.5_spmd} | conditional | flops 2214592000 | bytes 63332908 | solution.py:39
  255.2 5.0 fusion
  260.2 5.8 fusion.3
  266.0 5.5 fusion.2
  271.7 104.7 %all-gather.6.cloned.1.call-done = bf16[4,128,4096]{2,0,1:T(4,128)(2,1)} async-done(((bf16[4,2,4096]{2,0,1:T(4,128)(2,1)}), bf16[4,128,4096]{2,0,1:T(4,128)(2,1)}) %all-gather.6.cloned.1.call-update) | async-done | bytes 4194320 | tf_op jit(solution)/shard_map/all_gather | solution.py:87
  376.3 8.0 fusion.8
  384.9 18.0 %reduce-window.6 = s32[64,8,128]{2,1,0:T(8,128)S(1)} reduce-window(s32[64,8,128]{2,1,0:T(8,128)S(1)} %fusion.35, s32[]{:T(128)} %constant.71.clone.1), window={size=1x1x128 pad=0_0x0_0x127_0}, to_apply=%region_7.8 | reduce-window | flops 8323072 | bytes 524292 | tf_op jit(solution)/shard_map/reduce-window
  403.7 92.3 %reduce-scatter.2.cloned.1.call-done = bf16[128,512]{1,0:T(8,128)(2,1)} async-done(((bf16[128,4096]{1,0:T(8,128)(2,1)}), bf16[128,512]{1,0:T(8,128)(2,1)}) %reduce-scatter.2.cloned.1.call-update) | async-done | bytes 131088 | tf_op jit(solution)/shard_map/reduce_scatter | solution.py:89
  496.0 1.0 multiply_reduce_fusion
  497.1 29.7 %psum.14 = f32[128]{0:T(128)S(1)} all-reduce(f32[128]{0:T(128)S(1)} %multiply_reduce_fusion), channel_id=1, replica_groups=mesh['ctx'=64,'exp'=8] {'exp'}, use_global_device_ids=true, to_apply=%region_11.12 | all-reduce | flops 128 | bytes 1024 | tf_op jit(solution)/shard_map/psum | solution.py:93
  526.7 1.4 convolution_convert_fusion.1
  528.3 62.0 %all_to_all.10 = bf16[64,10,512]{2,1,0:T(8,128)(2,1)} all-to-all(bf16[64,10,512]{2,1,0:T(8,128)(2,1)S(1)} %reshape.120), channel_id=1, replica_groups=mesh['ctx'=64,'exp'=8] {'ctx'}, dimensions={0} | all-to-all | bytes 1310720 | tf_op jit(solution)/shard_map/all_to_all | solution.py:116
  590.3 1.4 reshape.144
  591.7 2.5 convolution_convert_fusion
  594.2 228.4 %all-reduce.2.cloned.1.call-done = bf16[640,2,768]{2,0,1:T(8,128)(2,1)} async-done(((bf16[640,2,768]{2,0,1:T(8,128)(2,1)}), bf16[640,2,768]{2,0,1:T(8,128)(2,1)}) %all-reduce.2.cloned.1.call-update) | async-done | bytes 1966096 | tf_op jit(solution)/shard_map/psum | solution.py:123
  822.5 1.8 convert_element_type.143
  825.1 1.2 reshape.122
  826.3 9.2 %all-to-all-start.1 = ((bf16[64,10,512]{2,1,0:T(8,128)(2,1)}), bf16[64,10,512]{2,1,0:T(8,128)(2,1)S(1)}, u32[]{:S(2)}, u32[]{:S(2)}) async-start(bf16[64,10,512]{2,1,0:T(8,128)(2,1)} %reshape.122), calls=%async_computation.2 | async-start | bytes 2097152 | tf_op jit(solution)/shard_map/all_to_all | solution.py:129
  836.4 50.4 %all-to-all-done.1 = bf16[64,10,512]{2,1,0:T(8,128)(2,1)S(1)} async-done(((bf16[64,10,512]{2,1,0:T(8,128)(2,1)}), bf16[64,10,512]{2,1,0:T(8,128)(2,1)S(1)}, u32[]{:S(2)}, u32[]{:S(2)}) %all-to-all-start.1) | async-done | bytes 655392 | tf_op jit(solution)/shard_map/all_to_all | solution.py:129
  887.1 4.0 gather_fusion
  891.8 1.6 fusion.28
  (66 shorter events, 8.4 us)
Async XLA Ops:
  7.2 584.5 %copy-start = (bf16[1,512,2,768]{3,2,1,0:T(2,128)(2,1)S(1)}, bf16[1,512,2,768]{3,2,1,0:T(2,128)(2,1)}, u32[]{:S(2)}) copy-start(bf16[1,512,2,768]{3,2,1,0:T(2,128)(2,1)} %param.19) | copy-start | bytes 4718596
  7.2 129.1 %all-gather.8.cloned.1.call-start = ((), (), s32[]{:S(2)}) async-start(), calls=%async_computation.6 | async-start | bytes 2129920 | tf_op jit(solution)/shard_map/all_gather | solution.py:71
  8.9 246.1 %all-gather.10.cloned.1.call-start = ((), (), s32[]{:S(2)}) async-start(), calls=%async_computation.7 | async-start | bytes 2129920 | tf_op jit(solution)/shard_map/all_gather | solution.py:72
  10.5 365.8 %all-gather.6.cloned.1.call-start = ((), (), s32[]{:S(2)}) async-start(), calls=%async_computation.3 | async-start | bytes 4259840 | tf_op jit(solution)/shard_map/all_gather | solution.py:87
  12.1 483.9 %reduce-scatter.2.cloned.1.call-start = ((), (), s32[]{:S(2)}) async-start(), calls=%async_computation.4 | async-start | bytes 1179648 | tf_op jit(solution)/shard_map/reduce_scatter | solution.py:89
  255.2 5.0 copy-start.6
  271.5 113.1 %copy-start.4 = (s32[128,8]{0,1:T(8,128)S(1)}, s32[128,8]{0,1:T(8,128)}, u32[]{:S(2)}) copy-start(s32[128,8]{0,1:T(8,128)} %param.17) | copy-start | bytes 12292
  271.7 113.2 %copy-start.3 = (bf16[512,128]{1,0:T(8,128)(2,1)}, bf16[512,128]{1,0:T(8,128)(2,1)S(1)}, u32[]{:S(2)}) copy-start(bf16[512,128]{1,0:T(8,128)(2,1)S(1)} %divide_convert_fusion) | copy-start | bytes 393220
  376.3 119.7 %copy-start.1 = (bf16[128,512]{1,0:T(8,128)(2,1)S(1)}, bf16[128,512]{1,0:T(8,128)(2,1)}, u32[]{:S(2)}) copy-start(bf16[128,512]{1,0:T(8,128)(2,1)} %param.15) | copy-start | bytes 393220
  376.3 150.4 %copy-start.8 = (f32[512]{0:T(512)S(1)}, f32[512]{0:T(512)}, u32[]{:S(2)}) copy-start(f32[512]{0:T(512)} %param.16) | copy-start | bytes 6148
  384.4 438.2 %all-reduce.2.cloned.1.call-start = ((), (), s32[]{:S(2)}) async-start(), calls=%async_computation.5 | async-start | bytes 3932160 | tf_op jit(solution)/shard_map/psum | solution.py:123
  594.2 230.2 %copy-start.7 = (bf16[1,768,512]{2,1,0:T(8,128)(2,1)S(1)}, bf16[1,768,512]{2,1,0:T(8,128)(2,1)}, u32[]{:S(2)}) copy-start(bf16[1,768,512]{2,1,0:T(8,128)(2,1)} %param.20) | copy-start | bytes 2359300
  824.4 11.3 %copy-start.5 = (f32[128,8]{0,1:T(8,128)S(1)}, f32[128,8]{0,1:T(8,128)}, u32[]{:S(2)}) copy-start(f32[128,8]{0,1:T(8,128)} %param.18) | copy-start | bytes 12292
  826.3 60.5 %all-to-all-start.1 = ((bf16[64,10,512]{2,1,0:T(8,128)(2,1)}), bf16[64,10,512]{2,1,0:T(8,128)(2,1)S(1)}, u32[]{:S(2)}, u32[]{:S(2)}) async-start(bf16[64,10,512]{2,1,0:T(8,128)(2,1)} %reshape.122), calls=%async_computation.2 | async-start | bytes 2097152 | tf_op jit(solution)/shard_map/all_to_all | solution.py:129
  887.1 4.7 copy-start.2
Sparse Core Ops, SparseCore 0:
  10.7 125.5 all-gather.7
  138.4 116.4 all-gather.9
  257.7 118.5 all-gather.5
  384.5 111.4 reduce-scatter.1
  594.3 228.1 all-reduce.1
where the time goes:
time: 900 us
  waiting for transfers between devices  717 us (80%)
  blocking collectives  91.6 us (10%)
  other arithmetic  29.8 us (3%)
  matrix products  23.4 us (3%)
  between operations  14.7 us (2%)
  local copies, waits for them, and re-layouts  13.5 us (2%)
  starting transfers between devices  9.59 us (1%)
    psum x1, waiting for transfers between devices, body(): lax.psum(partial_sum.astype(jnp.bfloat16), 'exp').astype(jnp.float32)  228 us
    all_gather x1, waiting for transfers between devices, body(): lax.all_gather(key_local, 'ctx', axis=0, tiled=True)  123 us
    all_gather x1, waiting for transfers between devices, body(): lax.all_gather(value_local, 'ctx', axis=0, tiled=True)  119 us
    all_gather x1, waiting for transfers between devices, body(): whole_out = lax.all_gather(w_out, 'ctx', axis=1, tiled=True)  105 us
    reduce_scatter x1, waiting for transfers between devices, body(): lax.psum_scatter(projected.astype(jnp.bfloat16), 'exp', scatter_dimension...  92.3 us
    all_to_all x1, blocking collectives, body(): lax.all_to_all(outgoing, 'ctx', split_axis=0, concat_axis=0, tiled=True)  62 us
    all_to_all x1, waiting for transfers between devices, body(): lax.all_to_all(result, 'ctx', split_axis=0, concat_axis=0, tiled=True)  50.4 us
    psum x1, blocking collectives, body(): square_sum = lax.psum(jnp.sum(hidden_state * hidden_state, axis=1), 'exp')  29.7 us
  transfers between devices with their start and end apart: 6, of which 6 were waited for; matrix products, arithmetic and copies ran while one was open for 4% of the time, Pallas kernels for 0%

commit v1 on v0

--- a/solution.py
+++ b/solution.py
@@ -120,7 +120,9 @@
     partial_sum = jnp.einsum(
         "rd,dgf->rgf", row_block, w_gate_up[0], preferred_element_type=jnp.float32
     )
-    summed = lax.psum(partial_sum.astype(jnp.bfloat16), "exp").astype(jnp.float32)
+    summed = jnp.sum(lax.all_gather(partial_sum.astype(jnp.bfloat16), "exp"), axis=0).astype(
+        jnp.float32
+    )
     hidden_units = (jax.nn.silu(summed[:, 0]) * summed[:, 1]).astype(jnp.bfloat16)
     result = jnp.dot(hidden_units, w_down[0], preferred_element_type=jnp.float32).astype(
         jnp.bfloat16

time: 900 us -> 1200 us (1.33)
  waiting for transfers between devices: 717 us -> 982 us
  starting transfers between devices: 9.59 us -> 30.9 us
    all_gather x0 -> x1, waiting for transfers between devices: none -> 493 us  [body(): lax.all_gather(partial_sum.astype(jnp.bfloat16), 'exp')]
    psum x1 -> x0, waiting for transfers between devices: 228 us -> none  [body(): lax.psum(partial_sum.astype(jnp.bfloat16), 'exp').astype(jnp.float32)]
    all_to_all x1, starting transfers between devices: 9.2 us -> 30.5 us  [body(): lax.all_to_all(result, 'ctx', split_axis=0, concat_axis=0, tiled=True)]
  transfers between devices with their start and end apart: 6 -> 6, of which waited for: 6 -> 6; matrix products, arithmetic and copies ran while one was open for 4% -> 3% of each run, Pallas kernels for 0% -> 0%
where the time goes in v1:
time: 1200 us; the launch traced here: 1190 us
  waiting for transfers between devices  982 us (82%)
  blocking collectives  91.6 us (8%)
  other arithmetic  37 us (3%)
  starting transfers between devices  30.9 us (3%)
  matrix products  23.3 us (2%)
  between operations  14.7 us (1%)
  local copies, waits for them, and re-layouts  14.3 us (1%)
    all_gather x1, waiting for transfers between devices, body(): lax.all_gather(partial_sum.astype(jnp.bfloat16), 'exp')  493 us
    all_gather x1, waiting for transfers between devices, body(): lax.all_gather(key_local, 'ctx', axis=0, tiled=True)  123 us
    all_gather x1, waiting for transfers between devices, body(): lax.all_gather(value_local, 'ctx', axis=0, tiled=True)  119 us
    all_gather x1, waiting for transfers between devices, body(): whole_out = lax.all_gather(w_out, 'ctx', axis=1, tiled=True)  105 us
    reduce_scatter x1, waiting for transfers between devices, body(): lax.psum_scatter(projected.astype(jnp.bfloat16), 'exp', scatter_dimension...  92.3 us
    all_to_all x1, blocking collectives, body(): lax.all_to_all(outgoing, 'ctx', split_axis=0, concat_axis=0, tiled=True)  62 us
    all_to_all x1, waiting for transfers between devices, body(): lax.all_to_all(result, 'ctx', split_axis=0, concat_axis=0, tiled=True)  50.4 us
    all_to_all x1, starting transfers between devices, body(): lax.all_to_all(result, 'ctx', split_axis=0, concat_axis=0, tiled=True)  30.5 us
  transfers between devices with their start and end apart: 6, of which 6 were waited for; matrix products, arithmetic and copies ran while one was open for 3% of the time, Pallas kernels for 0%

profile of v1, /device:TPU:7, one launch (start us, length us, event | category | flops | bytes accessed | tf_op | source)
XLA Modules:
  0.0 1193.7 jit_solution(16482536256510242516)
XLA Ops:
  10.6 1.5 copy.72
  13.5 122.8 %all-gather.10.cloned.1.call-done = bf16[8192,1,128]{2,0,1:T(8,128)(2,1)} async-done(((bf16[128,1,128]{2,0,1:T(8,128)(2,1)}), bf16[8192,1,128]{2,0,1:T(8,128)(2,1)}) %all-gather.10.cloned.1.call-update) | async-done | bytes 2097168 | tf_op jit(solution)/shard_map/all_gather | solution.py:71
  136.3 118.7 %all-gather.12.cloned.1.call-done = bf16[8192,1,128]{2,0,1:T(8,128)(2,1)} async-done(((bf16[128,1,128]{2,0,1:T(8,128)(2,1)}), bf16[8192,1,128]{2,0,1:T(8,128)(2,1)}) %all-gather.12.cloned.1.call-update) | async-done | bytes 2097168 | tf_op jit(solution)/shard_map/all_gather | solution.py:72
  255.0 16.5 %conditional.1 = (f32[512]{0:T(512)S(1)}, f32[512,128]{1,0:T(8,128)S(1)}) conditional(s32[]{:T(128)} %convert_element_type.126, () %tuple.16, (s32[128]{0:T(128)S(1)}, bf16[128,4,128]{2,1,0:T(4,128)(2,1)}, bf16[8192,128]{1,0:T(8,128)(2,1)}, bf16[8192,128]{1,0:T(8,128)(2,1)}) %tuple.48), branch_computations={%region_1.2_spmd, %region_2.5_spmd} | conditional | flops 2214592000 | bytes 63332908 | solution.py:39
  255.2 5.0 fusion
  260.2 5.8 fusion.3
  266.0 5.5 fusion.2
  271.7 104.7 %all-gather.8.cloned.1.call-done = bf16[4,128,4096]{2,0,1:T(4,128)(2,1)} async-done(((bf16[4,2,4096]{2,0,1:T(4,128)(2,1)}), bf16[4,128,4096]{2,0,1:T(4,128)(2,1)}) %all-gather.8.cloned.1.call-update) | async-done | bytes 4194320 | tf_op jit(solution)/shard_map/all_gather | solution.py:87
  376.3 8.0 fusion.8
  384.9 18.0 %reduce-window.6 = s32[64,8,128]{2,1,0:T(8,128)S(1)} reduce-window(s32[64,8,128]{2,1,0:T(8,128)S(1)} %fusion.35, s32[]{:T(128)} %constant.72.clone.1), window={size=1x1x128 pad=0_0x0_0x127_0}, to_apply=%region_7.8 | reduce-window | flops 8323072 | bytes 524292 | tf_op jit(solution)/shard_map/reduce-window
  403.7 92.3 %reduce-scatter.2.cloned.1.call-done = bf16[128,512]{1,0:T(8,128)(2,1)} async-done(((bf16[128,4096]{1,0:T(8,128)(2,1)}), bf16[128,512]{1,0:T(8,128)(2,1)}) %reduce-scatter.2.cloned.1.call-update) | async-done | bytes 131088 | tf_op jit(solution)/shard_map/reduce_scatter | solution.py:89
  496.0 1.0 multiply_reduce_fusion
  497.1 29.7 %psum.7 = f32[128]{0:T(128)S(1)} all-reduce(f32[128]{0:T(128)S(1)} %multiply_reduce_fusion), channel_id=1, replica_groups=mesh['ctx'=64,'exp'=8] {'exp'}, use_global_device_ids=true, to_apply=%region_11.12 | all-reduce | flops 128 | bytes 1024 | tf_op jit(solution)/shard_map/psum | solution.py:93
  526.7 1.4 convolution_convert_fusion.1
  528.3 62.0 %all_to_all.10 = bf16[64,10,512]{2,1,0:T(8,128)(2,1)} all-to-all(bf16[64,10,512]{2,1,0:T(8,128)(2,1)S(1)} %reshape.120), channel_id=1, replica_groups=mesh['ctx'=64,'exp'=8] {'ctx'}, dimensions={0} | all-to-all | bytes 1310720 | tf_op jit(solution)/shard_map/all_to_all | solution.py:116
  590.3 1.4 reshape.145
  591.7 2.5 convolution_convert_fusion
  594.2 492.8 %all-gather.14.cloned.1.call-done = bf16[5120,2,768]{2,0,1:T(8,128)(2,1)} async-done(((bf16[640,2,768]{2,0,1:T(8,128)(2,1)}), bf16[5120,2,768]{2,0,1:T(8,128)(2,1)}) %all-gather.14.cloned.1.call-update) | async-done | bytes 15728656 | tf_op jit(solution)/shard_map/all_gather | solution.py:123
  1086.9 8.8 reduce_sum.54
  1097.6 1.2 reshape.122
  1098.8 30.5 %all-to-all-start.1 = ((bf16[64,10,512]{2,1,0:T(8,128)(2,1)}), bf16[64,10,512]{2,1,0:T(8,128)(2,1)S(1)}, u32[]{:S(2)}, u32[]{:S(2)}) async-start(bf16[64,10,512]{2,1,0:T(8,128)(2,1)} %reshape.122), calls=%async_computation.2 | async-start | bytes 2097152 | tf_op jit(solution)/shard_map/all_to_all | solution.py:131
  1130.2 50.4 %all-to-all-done.1 = bf16[64,10,512]{2,1,0:T(8,128)(2,1)S(1)} async-done(((bf16[64,10,512]{2,1,0:T(8,128)(2,1)}), bf16[64,10,512]{2,1,0:T(8,128)(2,1)S(1)}, u32[]{:S(2)}, u32[]{:S(2)}) %all-to-all-start.1) | async-done | bytes 655392 | tf_op jit(solution)/shard_map/all_to_all | solution.py:131
  1180.9 4.0 gather_fusion
  1185.6 1.6 fusion.28
  (69 shorter events, 9.5 us)
Async XLA Ops:
  7.2 584.5 %copy-start = (bf16[1,512,2,768]{3,2,1,0:T(2,128)(2,1)S(1)}, bf16[1,512,2,768]{3,2,1,0:T(2,128)(2,1)}, u32[]{:S(2)}) copy-start(bf16[1,512,2,768]{3,2,1,0:T(2,128)(2,1)} %param.19) | copy-start | bytes 4718596
  7.2 129.1 %all-gather.10.cloned.1.call-start = ((), (), s32[]{:S(2)}) async-start(), calls=%async_computation.5 | async-start | bytes 2129920 | tf_op jit(solution)/shard_map/all_gather | solution.py:71
  8.9 246.1 %all-gather.12.cloned.1.call-start = ((), (), s32[]{:S(2)}) async-start(), calls=%async_computation.6 | async-start | bytes 2129920 | tf_op jit(solution)/shard_map/all_gather | solution.py:72
  10.5 365.8 %all-gather.8.cloned.1.call-start = ((), (), s32[]{:S(2)}) async-start(), calls=%async_computation.3 | async-start | bytes 4259840 | tf_op jit(solution)/shard_map/all_gather | solution.py:87
  12.1 483.9 %reduce-scatter.2.cloned.1.call-start = ((), (), s32[]{:S(2)}) async-start(), calls=%async_computation.4 | async-start | bytes 1179648 | tf_op jit(solution)/shard_map/reduce_scatter | solution.py:89
  255.2 5.0 copy-start.7
  271.5 113.1 %copy-start.5 = (s32[128,8]{0,1:T(8,128)S(1)}, s32[128,8]{0,1:T(8,128)}, u32[]{:S(2)}) copy-start(s32[128,8]{0,1:T(8,128)} %param.17) | copy-start | bytes 12292
  271.7 113.2 %copy-start.4 = (bf16[512,128]{1,0:T(8,128)(2,1)}, bf16[512,128]{1,0:T(8,128)(2,1)S(1)}, u32[]{:S(2)}) copy-start(bf16[512,128]{1,0:T(8,128)(2,1)S(1)} %divide_convert_fusion) | copy-start | bytes 393220
  376.3 119.7 %copy-start.1 = (bf16[128,512]{1,0:T(8,128)(2,1)S(1)}, bf16[128,512]{1,0:T(8,128)(2,1)}, u32[]{:S(2)}) copy-start(bf16[128,512]{1,0:T(8,128)(2,1)} %param.15) | copy-start | bytes 393220
  376.3 150.4 %copy-start.9 = (f32[512]{0:T(512)S(1)}, f32[512]{0:T(512)}, u32[]{:S(2)}) copy-start(f32[512]{0:T(512)} %param.16) | copy-start | bytes 6148
  384.4 702.6 %all-gather.14.cloned.1.call-start = ((), (), s32[]{:S(2)}) async-start(), calls=%async_computation.7 | async-start | bytes 17694720 | tf_op jit(solution)/shard_map/all_gather | solution.py:123
  1095.7 1.1 copy-start.8
  1096.9 32.7 %copy-start.6 = (f32[128,8]{0,1:T(8,128)S(1)}, f32[128,8]{0,1:T(8,128)}, u32[]{:S(2)}) copy-start(f32[128,8]{0,1:T(8,128)} %param.18) | copy-start | bytes 12292
  1098.8 81.9 %all-to-all-start.1 = ((bf16[64,10,512]{2,1,0:T(8,128)(2,1)}), bf16[64,10,512]{2,1,0:T(8,128)(2,1)S(1)}, u32[]{:S(2)}, u32[]{:S(2)}) async-start(bf16[64,10,512]{2,1,0:T(8,128)(2,1)} %reshape.122), calls=%async_computation.2 | async-start | bytes 2097152 | tf_op jit(solution)/shard_map/all_to_all | solution.py:131
  1180.9 4.7 copy-start.2
  1180.9 4.7 copy-start.3
Sparse Core Ops, SparseCore 0:
  10.7 125.5 all-gather.9
  138.4 116.4 all-gather.11
  257.7 118.5 all-gather.7
  384.5 111.4 reduce-scatter.1
  594.3 492.5 all-gather.13
